TPU v7x, 512 devices: a whole 4x8x8 slice. The times are simulated.
512 devices in a mesh: band: 8 (over y), gy: 8 (over z), gz: 8 (over x, core).
Axes of the slice: x: 4, y: 8, z: 8, core: 2. Of those that a mesh axis runs over, the one named last changes fastest.
Arguments:
- orbitals: float32 [1024, 48, 3840], P('band', 'gy', 'gz'), may hold values from -6 to 6
- occupied: bfloat16 [1024, 48, 3840], P('band', 'gy', 'gz'), may hold values from -6 to 6
- eigen: float32 [1024], P('band'), may hold values from -1.5 to 0
- potential: float32 [48, 3840], P('gy', 'gz'), may hold values from -2 to 0.5
- perturbation: float32 [48, 3840], P('gy', 'gz'), may hold values from 0.2 to 1.5
- precondition: float32 [48, 3840], P('gy', 'gz'), may hold values from 0.05 to 0.3
Outputs:
- updated: float32 [1024, 48, 3840], P('band', 'gy', 'gz')
- resid_norm: float32 [1024], P('band')
All inputs are finite; a program needn't handle non-finite values.
Results may differ from a plain program's by a relative error of at most 0.0008.
Values may be sent and summed in bfloat16 or wider, within the bound.
A program may use at most 128 MiB of HBM per device.

v0:
```python
import jax
import jax.numpy as jnp
from jax import lax
from jax.sharding import PartitionSpec as P

NX = 80
stencil = (-205.0 / 72.0, 8.0 / 5.0, -1.0 / 5.0, 8.0 / 315.0, -1.0 / 560.0)


def extended(block, sides, width):
    for axis, dim in sides:
        count = lax.axis_size(axis)
        forward = [(i, i + 1) for i in range(count - 1)]
        forward.append((count - 1, 0))
        backward = [(target, source) for source, target in forward]
        low = lax.ppermute(
            lax.slice_in_dim(block, block.shape[dim] - width, None, axis=dim), axis, forward
        )
        high = lax.ppermute(lax.slice_in_dim(block, 0, width, axis=dim), axis, backward)
        block = jnp.concatenate([low, block, high], axis=dim)
    return block


def along_x(field, dist):
    flat = field.shape[-1]
    position = lax.broadcasted_iota(jnp.int32, (flat,), 0) % NX
    lower = jnp.where(position >= dist, jnp.roll(field, dist, -1), jnp.roll(field, dist - NX, -1))
    upper = jnp.where(
        position < NX - dist, jnp.roll(field, -dist, -1), jnp.roll(field, NX - dist, -1)
    )
    return lower + upper


def laplace(field):
    rows_y = field.shape[1]
    flat = field.shape[2]
    padded_y = extended(field, (("gy", 1),), 4)
    padded_z = extended(field, (("gz", 2),), 4 * NX)
    total = 3.0 * stencil[0] * field
    for dist in range(1, 5):
        pair_y = (
            padded_y[:, 4 + dist : 4 + dist + rows_y, :]
            + padded_y[:, 4 - dist : 4 - dist + rows_y, :]
        )
        pair_z = (
            padded_z[:, :, (4 + dist) * NX : (4 + dist) * NX + flat]
            + padded_z[:, :, (4 - dist) * NX : (4 - dist) * NX + flat]
        )
        total = total + stencil[dist] * (along_x(field, dist) + pair_y + pair_z)
    return total


def on_device(orbitals, occupied, eigen, potential, perturbation, precondition):
    band_rows, rows_y, flat = orbitals.shape
    cells = NX * rows_y * lax.axis_size("gy") * (flat // NX) * lax.axis_size("gz")
    occ_wide = occupied.astype(jnp.float32)
    resid = (
        -0.5 * laplace(orbitals)
        + (potential[None] - eigen[:, None, None]) * orbitals
        + perturbation[None] * occ_wide
    )
    squares = jnp.sum(resid * resid, axis=(1, 2))
    squares = lax.psum(squares, ("gy", "gz"))
    trial = orbitals - precondition[None] * resid
    trial_low = trial.astype(jnp.bfloat16)
    partial_margins = jnp.einsum(
        "oyc,ryc->or",
        lax.all_gather(occupied, "band", axis=0, tiled=True),
        trial_low,
        preferred_element_type=jnp.float32,
    )
    margins = lax.psum(partial_margins, ("gy", "gz"))
    norms = jnp.sqrt(squares / cells + 1e-06)
    coeff = (margins / cells).astype(jnp.bfloat16)
    correction = jnp.einsum(
        "or,oyc->ryc",
        coeff,
        lax.all_gather(occupied, "band", axis=0, tiled=True),
        preferred_element_type=jnp.float32,
    )
    updated = trial - correction
    return (updated, norms)


def solution(mesh):
    placed = (
        P("band", "gy", "gz"),
        P("band", "gy", "gz"),
        P("band"),
        P("gy", "gz"),
        P("gy", "gz"),
        P("gy", "gz"),
    )
    return jax.shard_map(
        on_device,
        mesh=mesh,
        in_specs=placed,
        out_specs=(P("band", "gy", "gz"), P("band")),
        check_vma=False,
    )
```

profile of v0, /device:TPU:8, one launch (start us, length us, event | category | flops | bytes accessed | tf_op | source)
XLA Modules:
  0.0 306.1 jit_solution(4770405374905059568)
XLA Ops:
  7.2 0.0 all-gather.2.cloned.1.call-start
  7.2 0.7 all-gather.2.cloned.1.call-update
  7.9 0.0 copy-start
  7.9 0.0 all-reduce.2.cloned.1.call-start
  8.0 1.7 fusion.56
  9.7 4.3 %collective-permute-start.1 = (f32[128,4,480]{0,2,1:T(8,128)S(1)}, f32[128,4,480]{0,2,1:T(8,128)S(1)}, u32[]{:S(2)}, u32[]{:S(2)}) collective-permute-start(f32[128,4,480]{0,2,1:T(8,128)S(1)} %get-tuple-element.37), channel_id=1, source_target_pairs={{0,8},{8,16},{16,24},{24,32},{32,40},{40,48},{48,56},{56,0},{1,9},... | collective-permute-start | bytes 2949128 | tf_op jit(solution)/shard_map/ppermute | solution.py:16
  14.0 0.0 copy-done
  14.0 0.2 fusion.57
  14.2 0.0 collective-permute-start.3
  14.2 8.6 %collective-permute-start = (f32[128,4,480]{0,2,1:T(8,128)S(1)}, f32[128,4,480]{0,2,1:T(8,128)S(1)}, u32[]{:S(2)}, u32[]{:S(2)}) collective-permute-start(f32[128,4,480]{0,2,1:T(8,128)S(1)} %get-tuple-element.36), channel_id=1, source_target_pairs={{8,0},{16,8},{24,16},{32,24},{40,32},{48,40},{56,48},{0,56},{9,1},... | collective-permute-start | bytes 2949128 | tf_op jit(solution)/shard_map/ppermute | solution.py:19
  22.8 2.7 collective-permute-start.2
  25.4 0.6 fusion.40
  26.1 0.8 fusion.47
  27.0 0.8 fusion.51
  27.8 0.9 fusion.55
  28.7 1.2 fusion.46
  29.9 1.6 fusion.50
  31.5 1.9 fusion.45
  33.4 1.9 fusion.49
  35.3 1.8 fusion.53
  37.1 1.8 fusion.41
  38.9 0.5 fusion.29
  39.4 0.6 fusion.31
  40.0 1.6 fusion.54
  41.6 0.6 fusion.33
  42.2 0.5 fusion.35
  42.7 1.6 fusion.42
  44.4 0.0 collective-permute-done.1
  44.4 0.1 constant_dynamic-update-slice_fusion.3
  44.4 0.0 collective-permute-done.3
  44.5 0.1 constant_dynamic-update-slice_fusion.7
  44.5 0.6 constant_dynamic-update-slice_fusion.1
  45.2 0.0 collective-permute-done
  45.2 0.1 constant_dynamic-update-slice_fusion
  45.2 0.0 copy-start.2
  45.3 0.0 copy-start.3
  45.3 0.0 collective-permute-done.2
  45.3 0.1 constant_dynamic-update-slice_fusion.4
  45.4 0.6 copy-done.2
  46.0 0.0 copy-done.3
  46.0 0.0 copy-start.1
  46.0 13.7 %multiply_reduce_fusion = (f32[128]{0:T(128)}, f32[128,6,480]{0,2,1:T(8,128)S(1)}) fusion(bf16[128,6,480]{0,2,1:T(8,128)(2,1)} %param.7, f32[6,480]{1,0:T(8,128)S(1)} %copy-done.2, f32[128,6,480]{0,2,1:T(8,128)S(1)} %copy-done, f32[128]{0:T(128)} %param.8, f32[6,480]{1,0:T(8,128)S(1)} %copy-done.3, f32[128,6,800]{0,2,1:T(8,128)S(1)} %get-tuple-element.39, ...), kind=kLoop, calls=%fused_computation.39 | loop fusion | flops 22855552 | bytes 50900224 | tf_op jit(solution)/shard_map/reduce_sum | solution.py:62
  59.7 35.2 %all-gather.2.cloned.1.call-done = bf16[1024,6,480]{0,2,1:T(8,128)(2,1)} async-done(((bf16[128,6,480]{0,2,1:T(8,128)(2,1)}), bf16[1024,6,480]{0,2,1:T(8,128)(2,1)}) %all-gather.2.cloned.1.call-update) | async-done | bytes 5898256 | tf_op jit(solution)/shard_map/all_gather | solution.py:68
  94.9 0.0 copy-done.1
  94.9 0.0 copy-start.4
  94.9 6.2 %convolution_bitcast_fusion = f32[1024,128]{1,0:T(8,128)} fusion(bf16[1024,6,480]{0,2,1:T(8,128)(2,1)} %all-gather.2.cloned.1.call-done, f32[128,6,480]{0,2,1:T(8,128)S(1)} %copy-done, f32[128,6,480]{0,2,1:T(8,128)S(1)} %get-tuple-element.3, f32[6,480]{1,0:T(8,128)S(1)} %copy-done.1), kind=kOutput, calls=%fused_computation.42 | convolution fusion | flops 756080640 | bytes 9383168 | tf_op jit(solution)/shard_map/oyc,ryc->or/dot_general | solution.py:66
  101.1 0.0 all-reduce.2.cloned.1.call-update
  101.1 0.0 copy-done.4
  101.1 125.7 %psum.15 = f32[128]{0:T(128)S(1)} all-reduce(f32[128]{0:T(128)S(1)} %copy-done.4), channel_id=1, replica_groups=mesh['band'=8,'gy'=8,'gz'=8] {'gy','gz'}, use_global_device_ids=true, to_apply=%region_2.3 | all-reduce | flops 128 | bytes 1024 | tf_op jit(solution)/shard_map/psum | solution.py:63
  226.8 0.5 add_sqrt_fusion
  227.3 66.2 %all-reduce.2.cloned.1.call-done = f32[1024,128]{1,0:T(8,128)} async-done(((f32[1024,128]{1,0:T(8,128)}), f32[1024,128]{1,0:T(8,128)}) %all-reduce.2.cloned.1.call-update) | async-done | bytes 524304 | tf_op jit(solution)/shard_map/psum | solution.py:72
  293.6 5.7 %convolution_subtract_fusion = f32[128,6,480]{0,2,1:T(8,128)} fusion(bf16[1024,6,480]{0,2,1:T(8,128)(2,1)} %all-gather.2.cloned.1.call-done, f32[128,6,480]{0,2,1:T(8,128)S(1)} %copy-done, f32[128,6,480]{0,2,1:T(8,128)S(1)} %get-tuple-element.3, f32[6,480]{1,0:T(8,128)S(1)} %copy-done.1, f32[1024,128]{1,0:T(8,128)} %all-reduce.2.cloned.1.call-done), kind=kOutput, calls=%fused_computation.41 | convolution fusion | flops 756342784 | bytes 10857728 | tf_op jit(solution)/shard_map/or,oyc->ryc/dot_general | solution.py:75
  (4 shorter events, 0.1 us)
Async XLA Ops:
  7.2 87.7 %all-gather.2.cloned.1.call-start = ((), (), s32[]{:S(2)}) async-start(), calls=%async_computation | async-start | bytes 6635520 | tf_op jit(solution)/shard_map/all_gather | solution.py:68
  7.9 6.1 %copy-start = (f32[128,6,480]{0,2,1:T(8,128)S(1)}, f32[128,6,480]{0,2,1:T(8,128)}, u32[]{:S(2)}) copy-start(f32[128,6,480]{0,2,1:T(8,128)} %param.6) | copy-start | bytes 4423684
  7.9 285.7 %all-reduce.2.cloned.1.call-start = ((), (), s32[]{:S(2)}) async-start(), calls=%async_computation.1 | async-start | bytes 1048576 | tf_op jit(solution)/shard_map/psum | solution.py:72
  9.7 34.7 %collective-permute-start.1 = (f32[128,4,480]{0,2,1:T(8,128)S(1)}, f32[128,4,480]{0,2,1:T(8,128)S(1)}, u32[]{:S(2)}, u32[]{:S(2)}) collective-permute-start(f32[128,4,480]{0,2,1:T(8,128)S(1)} %get-tuple-element.37), channel_id=1, source_target_pairs={{0,8},{8,16},{16,24},{24,32},{32,40},{40,48},{48,56},{56,0},{1,9},... | collective-permute-start | bytes 2949128 | tf_op jit(solution)/shard_map/ppermute | solution.py:16
  14.2 30.3 %collective-permute-start.3 = (f32[128,6,320]{0,2,1:T(8,128)S(1)}, f32[128,6,320]{0,2,1:T(8,128)S(1)}, u32[]{:S(2)}, u32[]{:S(2)}) collective-permute-start(f32[128,6,320]{0,2,1:T(8,128)S(1)} %get-tuple-element.43), channel_id=1, source_target_pairs={{0,1},{1,2},{2,3},{3,4},{4,5},{5,6},{6,7},{7,0},{8,9},{9,10},{10,1... | collective-permute-start | bytes 2949128 | tf_op jit(solution)/shard_map/ppermute | solution.py:16
  14.2 31.0 %collective-permute-start = (f32[128,4,480]{0,2,1:T(8,128)S(1)}, f32[128,4,480]{0,2,1:T(8,128)S(1)}, u32[]{:S(2)}, u32[]{:S(2)}) collective-permute-start(f32[128,4,480]{0,2,1:T(8,128)S(1)} %get-tuple-element.36), channel_id=1, source_target_pairs={{8,0},{16,8},{24,16},{32,24},{40,32},{48,40},{56,48},{0,56},{9,1},... | collective-permute-start | bytes 2949128 | tf_op jit(solution)/shard_map/ppermute | solution.py:19
  22.8 22.5 %collective-permute-start.2 = (f32[128,6,320]{0,2,1:T(8,128)S(1)}, f32[128,6,320]{0,2,1:T(8,128)S(1)}, u32[]{:S(2)}, u32[]{:S(2)}) collective-permute-start(f32[128,6,320]{0,2,1:T(8,128)S(1)} %get-tuple-element.42), channel_id=1, source_target_pairs={{1,0},{2,1},{3,2},{4,3},{5,4},{6,5},{7,6},{0,7},{9,8},{10,9},{11,1... | collective-permute-start | bytes 2949128 | tf_op jit(solution)/shard_map/ppermute | solution.py:19
  45.2 0.7 copy-start.2
  45.3 0.7 copy-start.3
  46.0 48.9 %copy-start.1 = (f32[6,480]{1,0:T(8,128)S(1)}, f32[6,480]{1,0:T(8,128)}, u32[]{:S(2)}) copy-start(f32[6,480]{1,0:T(8,128)} %param.11) | copy-start | bytes 34564
  94.9 6.3 %copy-start.4 = (f32[128]{0:T(128)S(1)}, f32[128]{0:T(128)}, u32[]{:S(2)}) copy-start(f32[128]{0:T(128)} %get-tuple-element.2) | copy-start | bytes 1540
Sparse Core Ops, SparseCore 0:
  10.0 84.8 all-gather.1
  101.2 192.2 all-reduce.1
where the time goes:
time: 306 us
  blocking collectives  126 us (41%)
  waiting for transfers between devices  102 us (33%)
  local copies, waits for them, and re-layouts  20.1 us (7%)
  other arithmetic  16.5 us (5%)
  starting transfers between devices  15.6 us (5%)
  between operations  14.2 us (5%)
  matrix products  11.9 us (4%)
    psum x1, blocking collectives, on_device(): squares = lax.psum(squares, ('gy', 'gz'))  126 us
    psum x1, waiting for transfers between devices, on_device(): margins = lax.psum(partial_margins, ('gy', 'gz'))  66.2 us
    all_gather x1, waiting for transfers between devices, on_device(): lax.all_gather(occupied, 'band', axis=0, tiled=True)  35.2 us
    reduce_sum x1, other arithmetic, on_device(): squares = jnp.sum(resid * resid, axis=(1, 2))  13.7 us
    ppermute x2, starting transfers between devices, extended(): lax.ppermute(lax.slice_in_dim(block, 0, width, axis=dim), axis, backward)  11.2 us
    slice x8, local copies, waits for them, and re-layouts, along_x(): jnp.roll(field, dist - NX, -1)  8.63 us
    slice x8, local copies, waits for them, and re-layouts, along_x(): jnp.roll(field, dist, -1)  8.03 us
    dot_general x1, matrix products, on_device(): jnp.einsum('oyc,ryc->or', lax.all_gather(occupied, 'band', axis=0, tiled=...  6.24 us
  transfers between devices with their start and end apart: 6, of which 2 were waited for; matrix products, arithmetic and copies ran while one was open for 12% of the time, Pallas kernels for 0%

commit v1 on v0

--- a/solution.py
+++ b/solution.py
@@ -69,7 +69,8 @@
         trial_low,
         preferred_element_type=jnp.float32,
     )
-    margins = lax.psum(partial_margins, ("gy", "gz"))
+    blocks = lax.all_gather(partial_margins, ("gy", "gz"), axis=0, tiled=False)
+    margins = blocks.sum(axis=0)
     norms = jnp.sqrt(squares / cells + 1e-06)
     coeff = (margins / cells).astype(jnp.bfloat16)
     correction = jnp.einsum(

time: 306 us -> 297 us (0.971)
  the two profiles are of different devices: /device:TPU:8 before, /device:TPU:1 now
where the time goes in v1:
time: 297 us
  blocking collectives  131 us (44%)
  waiting for transfers between devices  54.6 us (18%)
  local copies, waits for them, and re-layouts  48 us (16%)
  other arithmetic  23.2 us (8%)
  starting transfers between devices  15.3 us (5%)
  between operations  14.2 us (5%)
  matrix products  10.7 us (4%)
    psum x1, blocking collectives, on_device(): squares = lax.psum(squares, ('gy', 'gz'))  131 us
    unnamed x14, local copies, waits for them, and re-layouts  29.6 us
    all_gather x1, waiting for transfers between devices, on_device(): lax.all_gather(occupied, 'band', axis=0, tiled=True)  29 us
    all_gather x1, waiting for transfers between devices, on_device(): blocks = lax.all_gather(partial_margins, ('gy', 'gz'), axis=0, tiled=False)  20.6 us
    reduce_sum x1, other arithmetic, on_device(): squares = jnp.sum(resid * resid, axis=(1, 2))  13.6 us
    ppermute x2, starting transfers between devices, extended(): lax.ppermute(lax.slice_in_dim(block, 0, width, axis=dim), axis, backward)  13.3 us
    slice x8, local copies, waits for them, and re-layouts, along_x(): jnp.roll(field, dist - NX, -1)  8.5 us
    slice x8, local copies, waits for them, and re-layouts, along_x(): jnp.roll(field, dist, -1)  7.91 us
  transfers between devices with their start and end apart: 6, of which 3 were waited for; matrix products, arithmetic and copies ran while one was open for 12% of the time, Pallas kernels for 0%

profile of v1, /device:TPU:1, one launch (start us, length us, event | category | flops | bytes accessed | tf_op | source)
XLA Modules:
  0.0 296.6 jit_solution(7964956942114754367)
XLA Ops:
  7.2 0.0 all-gather.4.cloned.1.call-start
  7.2 0.7 all-gather.4.cloned.1.call-update
  7.9 0.0 copy-start
  7.9 0.0 all-gather.6.cloned.1.call-start
  8.0 1.7 fusion.57
  9.7 6.9 %collective-permute-start.2 = (f32[128,6,320]{0,2,1:T(8,128)S(1)}, f32[128,6,320]{0,2,1:T(8,128)S(1)}, u32[]{:S(2)}, u32[]{:S(2)}) collective-permute-start(f32[128,6,320]{0,2,1:T(8,128)S(1)} %get-tuple-element.42), channel_id=1, source_target_pairs={{1,0},{2,1},{3,2},{4,3},{5,4},{6,5},{7,6},{0,7},{9,8},{10,9},{11,1... | collective-permute-start | bytes 2949128 | tf_op jit(solution)/shard_map/ppermute | solution.py:19
  16.6 0.0 collective-permute-start.3
  16.6 0.0 copy-done
  16.6 0.1 fusion.56
  16.7 6.4 %collective-permute-start = (f32[128,4,480]{0,2,1:T(8,128)S(1)}, f32[128,4,480]{0,2,1:T(8,128)S(1)}, u32[]{:S(2)}, u32[]{:S(2)}) collective-permute-start(f32[128,4,480]{0,2,1:T(8,128)S(1)} %get-tuple-element.36), channel_id=1, source_target_pairs={{8,0},{16,8},{24,16},{32,24},{40,32},{48,40},{56,48},{0,56},{9,1},... | collective-permute-start | bytes 2949128 | tf_op jit(solution)/shard_map/ppermute | solution.py:19
  23.2 1.9 collective-permute-start.1
  25.1 0.6 fusion.40
  25.8 0.8 fusion.51
  26.6 0.8 fusion.47
  27.4 0.8 fusion.43
  28.3 1.2 fusion.46
  29.4 1.6 fusion.54
  31.1 1.8 fusion.45
  32.9 1.8 fusion.49
  34.7 1.9 fusion.41
  36.5 1.8 fusion.53
  38.4 0.5 fusion.35
  38.9 0.6 fusion.33
  39.5 1.6 fusion.50
  41.0 0.6 fusion.31
  41.6 0.6 fusion.29
  42.2 1.6 fusion.42
  43.8 0.0 collective-permute-done.3
  43.9 0.1 constant_dynamic-update-slice_fusion.7
  43.9 4.3 %collective-permute-done.1 = f32[128,4,480]{0,2,1:T(8,128)S(1)} collective-permute-done((f32[128,4,480]{0,2,1:T(8,128)S(1)}, f32[128,4,480]{0,2,1:T(8,128)S(1)}, u32[]{:S(2)}, u32[]{:S(2)}) %collective-permute-start.1) | collective-permute-done | bytes 983072 | tf_op jit(solution)/shard_map/ppermute | solution.py:16
  48.3 0.1 constant_dynamic-update-slice_fusion.3
  48.3 0.6 constant_dynamic-update-slice_fusion.1
  49.0 0.0 collective-permute-done
  49.0 0.1 constant_dynamic-update-slice_fusion
  49.0 0.0 copy-start.2
  49.1 0.0 copy-start.3
  49.1 0.0 collective-permute-done.2
  49.1 0.1 constant_dynamic-update-slice_fusion.4
  49.1 0.6 copy-done.2
  49.8 0.0 copy-done.3
  49.8 0.0 copy-start.1
  49.8 13.6 %multiply_reduce_fusion = (f32[128]{0:T(128)}, f32[128,6,480]{0,2,1:T(8,128)S(1)}) fusion(bf16[128,6,480]{0,2,1:T(8,128)(2,1)} %param.7, f32[6,480]{1,0:T(8,128)S(1)} %copy-done.2, f32[128,6,480]{0,2,1:T(8,128)S(1)} %copy-done, f32[128]{0:T(128)} %param.8, f32[6,480]{1,0:T(8,128)S(1)} %copy-done.3, f32[128,6,800]{0,2,1:T(8,128)S(1)} %get-tuple-element.39, ...), kind=kLoop, calls=%fused_computation.40 | loop fusion | flops 22855552 | bytes 50900224 | tf_op jit(solution)/shard_map/reduce_sum | solution.py:62
  63.4 29.0 %all-gather.4.cloned.1.call-done = bf16[1024,6,480]{0,2,1:T(8,128)(2,1)} async-done(((bf16[128,6,480]{0,2,1:T(8,128)(2,1)}), bf16[1024,6,480]{0,2,1:T(8,128)(2,1)}) %all-gather.4.cloned.1.call-update) | async-done | bytes 5898256 | tf_op jit(solution)/shard_map/all_gather | solution.py:68
  92.4 0.0 copy-done.1
  92.4 0.0 copy-start.4
  92.4 5.2 %convolution_bitcast_fusion = f32[1024,128]{0,1:T(8,128)} fusion(bf16[1024,6,480]{0,2,1:T(8,128)(2,1)} %all-gather.4.cloned.1.call-done, f32[128,6,480]{0,2,1:T(8,128)S(1)} %copy-done, f32[128,6,480]{0,2,1:T(8,128)S(1)} %get-tuple-element.3, f32[6,480]{1,0:T(8,128)S(1)} %copy-done.1), kind=kOutput, calls=%fused_computation.43 | convolution fusion | flops 756080640 | bytes 9383168 | tf_op jit(solution)/shard_map/oyc,ryc->or/dot_general | solution.py:66
  97.6 0.0 all-gather.6.cloned.1.call-update
  97.6 0.0 copy-done.4
  97.6 130.6 %psum.7 = f32[128]{0:T(128)S(1)} all-reduce(f32[128]{0:T(128)S(1)} %copy-done.4), channel_id=1, replica_groups=mesh['band'=8,'gy'=8,'gz'=8] {'gy','gz'}, use_global_device_ids=true, to_apply=%region_2.3 | all-reduce | flops 128 | bytes 1024 | tf_op jit(solution)/shard_map/psum | solution.py:63
  228.2 0.5 add_sqrt_fusion
  228.7 20.6 %all-gather.6.cloned.1.call-done = f32[65536,128]{0,1:T(8,128)} async-done(((f32[1024,128]{0,1:T(8,128)}), f32[65536,128]{0,1:T(8,128)}) %all-gather.6.cloned.1.call-update) | async-done | bytes 33554448 | tf_op jit(solution)/shard_map/all_gather | solution.py:72
  249.3 28.2 %copy.11 = f32[16,8,64,1024]{3,2,1,0:T(8,128)S(1)} copy(f32[16,8,64,1024]{3,1,2,0:T(8,128)} %bitcast.14) | data formatting | bytes 67108864
  277.6 6.7 %bitcast_reduce_fusion = f32[1024,128]{0,1:T(8,128)S(1)} fusion(f32[16,8,64,1024]{3,2,1,0:T(8,128)S(1)} %copy.11), kind=kLoop, calls=%fused_computation | loop fusion | flops 8257536 | bytes 34078720 | tf_op jit(solution)/shard_map/reduce_sum | solution.py:73
  284.3 5.5 %convolution_subtract_fusion = f32[128,6,480]{0,2,1:T(8,128)} fusion(bf16[1024,6,480]{0,2,1:T(8,128)(2,1)} %all-gather.4.cloned.1.call-done, f32[128,6,480]{0,2,1:T(8,128)S(1)} %copy-done, f32[128,6,480]{0,2,1:T(8,128)S(1)} %get-tuple-element.3, f32[6,480]{1,0:T(8,128)S(1)} %copy-done.1, f32[1024,128]{0,1:T(8,128)S(1)} %bitcast_reduce_fusion), kind=kOutput, calls=%fused_computation.42 | convolution fusion | flops 756342784 | bytes 10857728 | tf_op jit(solution)/shard_map/or,oyc->ryc/dot_general | solution.py:76
  (4 shorter events, 0.1 us)
Async XLA Ops:
  7.2 85.2 %all-gather.4.cloned.1.call-start = ((), (), s32[]{:S(2)}) async-start(), calls=%async_computation | async-start | bytes 6635520 | tf_op jit(solution)/shard_map/all_gather | solution.py:68
  7.9 8.7 %copy-start = (f32[128,6,480]{0,2,1:T(8,128)S(1)}, f32[128,6,480]{0,2,1:T(8,128)}, u32[]{:S(2)}) copy-start(f32[128,6,480]{0,2,1:T(8,128)} %param.6) | copy-start | bytes 4423684
  7.9 241.4 %all-gather.6.cloned.1.call-start = ((), (), s32[]{:S(2)}) async-start(), calls=%async_computation.1 | async-start | bytes 34078720 | tf_op jit(solution)/shard_map/all_gather | solution.py:72
  9.7 39.4 %collective-permute-start.2 = (f32[128,6,320]{0,2,1:T(8,128)S(1)}, f32[128,6,320]{0,2,1:T(8,128)S(1)}, u32[]{:S(2)}, u32[]{:S(2)}) collective-permute-start(f32[128,6,320]{0,2,1:T(8,128)S(1)} %get-tuple-element.42), channel_id=1, source_target_pairs={{1,0},{2,1},{3,2},{4,3},{5,4},{6,5},{7,6},{0,7},{9,8},{10,9},{11,1... | collective-permute-start | bytes 2949128 | tf_op jit(solution)/shard_map/ppermute | solution.py:19
  16.6 27.3 %collective-permute-start.3 = (f32[128,6,320]{0,2,1:T(8,128)S(1)}, f32[128,6,320]{0,2,1:T(8,128)S(1)}, u32[]{:S(2)}, u32[]{:S(2)}) collective-permute-start(f32[128,6,320]{0,2,1:T(8,128)S(1)} %get-tuple-element.43), channel_id=1, source_target_pairs={{0,1},{1,2},{2,3},{3,4},{4,5},{5,6},{6,7},{7,0},{8,9},{9,10},{10,1... | collective-permute-start | bytes 2949128 | tf_op jit(solution)/shard_map/ppermute | solution.py:16
  16.7 32.2 %collective-permute-start = (f32[128,4,480]{0,2,1:T(8,128)S(1)}, f32[128,4,480]{0,2,1:T(8,128)S(1)}, u32[]{:S(2)}, u32[]{:S(2)}) collective-permute-start(f32[128,4,480]{0,2,1:T(8,128)S(1)} %get-tuple-element.36), channel_id=1, source_target_pairs={{8,0},{16,8},{24,16},{32,24},{40,32},{48,40},{56,48},{0,56},{9,1},... | collective-permute-start | bytes 2949128 | tf_op jit(solution)/shard_map/ppermute | solution.py:19
  23.2 25.1 %collective-permute-start.1 = (f32[128,4,480]{0,2,1:T(8,128)S(1)}, f32[128,4,480]{0,2,1:T(8,128)S(1)}, u32[]{:S(2)}, u32[]{:S(2)}) collective-permute-start(f32[128,4,480]{0,2,1:T(8,128)S(1)} %get-tuple-element.37), channel_id=1, source_target_pairs={{0,8},{8,16},{16,24},{24,32},{32,40},{40,48},{48,56},{56,0},{1,9},... | collective-permute-start | bytes 2949128 | tf_op jit(solution)/shard_map/ppermute | solution.py:16
  49.0 0.7 copy-start.2
  49.1 0.7 copy-start.3
  49.8 42.6 %copy-start.1 = (f32[6,480]{1,0:T(8,128)S(1)}, f32[6,480]{1,0:T(8,128)}, u32[]{:S(2)}) copy-start(f32[6,480]{1,0:T(8,128)} %param.11) | copy-start | bytes 34564
  92.4 5.2 %copy-start.4 = (f32[128]{0:T(128)S(1)}, f32[128]{0:T(128)}, u32[]{:S(2)}) copy-start(f32[128]{0:T(128)} %get-tuple-element.2) | copy-start | bytes 1540
Sparse Core Ops, SparseCore 0:
  10.0 82.3 all-gather.3
  97.7 151.5 all-gather.5
